TPU v7x, 32 devices: a whole 2x2x4 slice. The times are simulated.
32 devices in a mesh: clips: 2 (over y), ctx: 4 (over z), head: 4 (over x, core).
Axes of the slice: x: 2, y: 2, z: 4, core: 2. Of those that a mesh axis runs over, the one named last changes fastest.
Arguments:
- queries: bfloat16 [9216, 1536], P(('clips', 'ctx', 'head')), parts along dimension 0
- keys: bfloat16 [9216, 1536], P(('clips', 'ctx', 'head')), parts along dimension 0
- values: bfloat16 [9216, 1536], P(('clips', 'ctx', 'head')), parts along dimension 0, may hold values from -4.5 to 4.5
- neighbors: int32 [24, 8], P(('clips', 'ctx')), parts along dimension 0, may hold values from 0 to 11, as said below
- tile_counts: int32 [24], P(('clips', 'ctx')), parts along dimension 0, may hold values from 192 to 384
Outputs:
- attended: bfloat16 [9216, 1536], P(('clips', 'ctx', 'head')), parts along dimension 0
There are 2 independent parts, one for each index of `clips`. A program takes and returns all parts, laid end to end along the dimension named above; each array names one. Nothing has to cross between parts.
Inputs may be any that keep to these rules, and one draw needn't show every extreme that they name: `neighbors`: row t starts with t itself, followed by 8 - 1 distinct other tiles of t's 3 x 3 x 3 window of tiles: frame layer, row and column each differ from t's by at most one.
All inputs are finite; a program needn't handle non-finite values.
Results may differ from a plain program's by a relative error of at most 0.0049.
Values may be sent and summed in bfloat16 or wider, within the bound.
A program may use at most 64 MiB of HBM per device.

v0:
```python
import jax
import jax.numpy as jnp
from jax import lax
from jax.sharding import PartitionSpec as P

DH = 128
TILE = 384
NB = 8
REACH = 10
HOPS = 4


def shifted(array, axis, by):
    peers = lax.axis_size(axis)
    pairs = [(i, i + by) for i in range(peers) if 0 <= i + by < peers]
    return lax.ppermute(array, axis, pairs)


def join_pieces(pieces):
    return tuple(
        (jnp.concatenate([piece[member] for piece in pieces], axis=0) for member in range(3))
    )


def shards(queries, keys, values, neighbors, tile_counts):
    block_queries, block_keys, block_values = (
        lax.all_to_all(queries, "head", split_axis=1, concat_axis=0, tiled=True),
        lax.all_to_all(keys, "head", split_axis=1, concat_axis=0, tiled=True),
        lax.all_to_all(values, "head", split_axis=1, concat_axis=0, tiled=True),
    )
    tiles_here = tile_counts.shape[0]
    local_width = block_queries.shape[1]
    local_heads = local_width // DH
    earlier = []
    later = []
    for distance in range(1, HOPS + 1):
        taken = min(tiles_here, REACH - (distance - 1) * tiles_here)
        rows_taken = taken * TILE
        sent_back = (block_keys[-rows_taken:], block_values[-rows_taken:], tile_counts[-taken:])
        earlier = [shifted((sent_back[0], sent_back[1], sent_back[2]), "ctx", distance)] + earlier
        sent_fore = (block_keys[:rows_taken], block_values[:rows_taken], tile_counts[:taken])
        later = later + [shifted((sent_fore[0], sent_fore[1], sent_fore[2]), "ctx", -distance)]
    before = join_pieces(earlier)
    after = join_pieces(later)
    ext_tiles = tiles_here + 2 * REACH
    ext_keys = jnp.concatenate([before[0], block_keys, after[0]], axis=0).reshape(
        ext_tiles, TILE, local_width
    )
    ext_values = jnp.concatenate([before[1], block_values, after[1]], axis=0).reshape(
        ext_tiles, TILE, local_width
    )
    ext_counts = jnp.concatenate([before[2], tile_counts, after[2]], axis=0)
    slot_index = jnp.arange(TILE, dtype=jnp.int32)
    key_live = slot_index[None, :] < ext_counts[:, None]
    first_tile = lax.axis_index("ctx") * tiles_here - REACH
    local_lists = jnp.clip(neighbors - first_tile, 0, ext_tiles - 1)
    query_tiles = block_queries.reshape(tiles_here, TILE, local_width)

    def one_tile(tile_index):
        query_block = query_tiles[tile_index]
        listed = local_lists[tile_index]
        key_block = ext_keys[listed].reshape(NB * TILE, local_width)
        value_block = ext_values[listed].reshape(NB * TILE, local_width)
        key_mask = key_live[listed].reshape(NB * TILE)

        def one_head(head_index, result):
            start = head_index * DH
            query_rows = lax.dynamic_slice_in_dim(query_block, start, DH, 1)
            key_rows = lax.dynamic_slice_in_dim(key_block, start, DH, 1)
            value_rows = lax.dynamic_slice_in_dim(value_block, start, DH, 1)
            scores = lax.dot_general(
                query_rows, key_rows, (((1,), (1,)), ((), ())), preferred_element_type=jnp.float32
            ) * DH ** (-0.5)
            scores = jnp.where(key_mask[None, :], scores, -jnp.inf)
            highest = jnp.max(scores, axis=1, keepdims=True)
            weights = jnp.exp(scores - highest)
            totals = jnp.sum(weights, axis=1, keepdims=True)
            rounded = weights.astype(jnp.bfloat16)
            summed = jnp.dot(rounded, value_rows, preferred_element_type=jnp.float32)
            head_out = (summed / totals).astype(jnp.bfloat16)
            return lax.dynamic_update_slice_in_dim(result, head_out, start, 1)

        empty = jnp.zeros((TILE, local_width), jnp.bfloat16)
        return lax.fori_loop(0, local_heads, one_head, empty)

    outputs = lax.map(one_tile, jnp.arange(tiles_here, dtype=jnp.int32))
    outputs = outputs.reshape(tiles_here * TILE, local_width)
    return lax.all_to_all(outputs, "head", split_axis=0, concat_axis=1, tiled=True)


def solution(mesh):
    placed = (
        P(("clips", "ctx", "head"), None),
        P(("clips", "ctx", "head"), None),
        P(("clips", "ctx", "head"), None),
        P(("clips", "ctx"), None),
        P(("clips", "ctx")),
    )
    return jax.shard_map(
        shards,
        mesh=mesh,
        in_specs=placed,
        out_specs=P(("clips", "ctx", "head"), None),
        check_vma=False,
    )
```

profile of v0, /device:TPU:0, one launch (start us, length us, event | category | flops | bytes accessed | tf_op | source)
XLA Modules:
  0.0 357.6 jit_solution(14620852755360953468)
XLA Ops:
  0.0 2.2 copy.22
  2.3 4.2 %all-to-all-start.2 = ((bf16[288,4,384]{2,0,1:T(8,128)(2,1)}), bf16[288,4,384]{2,0,1:T(8,128)(2,1)S(1)}, u32[]{:S(2)}, u32[]{:S(2)}) async-start(bf16[288,4,384]{2,0,1:T(8,128)(2,1)} %bitcast.39), calls=%async_computation.2 | async-start | bytes 1769472 | tf_op jit(solution)/shard_map/all_to_all | solution.py:29
  6.5 2.2 copy.23
  8.7 10.5 %all-to-all-done.2 = bf16[288,4,384]{2,0,1:T(8,128)(2,1)S(1)} async-done(((bf16[288,4,384]{2,0,1:T(8,128)(2,1)}), bf16[288,4,384]{2,0,1:T(8,128)(2,1)S(1)}, u32[]{:S(2)}, u32[]{:S(2)}) %all-to-all-start.2) | async-done | bytes 884768 | tf_op jit(solution)/shard_map/all_to_all | solution.py:29
  19.2 3.5 all-to-all-start.1
  22.7 6.2 %collective-permute-start.17 = (s32[3]{0:T(128)S(1)}, s32[3]{0:T(128)S(1)}, u32[]{:S(2)}, u32[]{:S(2)}) collective-permute-start(s32[3]{0:T(128)S(1)} %copy-done.4), channel_id=1, source_target_pairs={{0,12},{1,13},{2,14},{3,15},{16,28},{17,29},{18,30},{19,31}} | collective-permute-start | bytes 44 | tf_op jit(solution)/shard_map/ppermute | solution.py:16
  29.5 1.2 collective-permute-start.16
  31.8 1.3 collective-permute-start.9
  33.1 1.3 collective-permute-start.10
  35.3 1.4 collective-permute-start.8
  36.7 4.2 %all-to-all-start = ((bf16[288,4,384]{2,0,1:T(8,128)(2,1)}), bf16[288,4,384]{2,0,1:T(8,128)(2,1)}, u32[]{:S(2)}, u32[]{:S(2)}) async-start(bf16[288,4,384]{2,0,1:T(8,128)(2,1)} %bitcast.41), calls=%async_computation | async-start | bytes 1769472 | tf_op jit(solution)/shard_map/all_to_all | solution.py:27
  41.9 1.2 collective-permute-start.23
  43.1 3.8 %collective-permute-start.18 = (s32[3]{0:T(128)S(1)}, s32[3]{0:T(128)S(1)}, u32[]{:S(2)}, u32[]{:S(2)}) collective-permute-start(s32[3]{0:T(128)S(1)} %copy-done.4), channel_id=1, source_target_pairs={{0,8},{4,12},{1,9},{5,13},{2,10},{6,14},{3,11},{7,15},{16,24},{20,... | collective-permute-start | bytes 44 | tf_op jit(solution)/shard_map/ppermute | solution.py:16
  46.9 3.5 collective-permute-start.19
  50.4 21.2 %collective-permute-done.18 = s32[3]{0:T(128)S(1)} collective-permute-done((s32[3]{0:T(128)S(1)}, s32[3]{0:T(128)S(1)}, u32[]{:S(2)}, u32[]{:S(2)}) %collective-permute-start.18) | collective-permute-done | bytes 44 | tf_op jit(solution)/shard_map/ppermute | solution.py:16
  71.6 1.3 collective-permute-start.20
  72.9 1.3 collective-permute-start.21
  74.2 21.3 %collective-permute-done.20 = s32[3]{0:T(128)S(1)} collective-permute-done((s32[3]{0:T(128)S(1)}, s32[3]{0:T(128)S(1)}, u32[]{:S(2)}, u32[]{:S(2)}) %collective-permute-start.20) | collective-permute-done | bytes 44 | tf_op jit(solution)/shard_map/ppermute | solution.py:16
  95.5 1.3 collective-permute-start.22
  96.8 1.5 collective-permute-done.21
  98.2 4.9 %collective-permute-start.11 = (bf16[1152,384]{1,0:T(8,128)(2,1)S(1)}, bf16[1152,384]{1,0:T(8,128)(2,1)}, u32[]{:S(2)}, u32[]{:S(2)}) collective-permute-start(bf16[1152,384]{1,0:T(8,128)(2,1)S(1)} %bitcast.69), channel_id=1, source_target_pairs={{0,4},{4,8},{8,12},{1,5},{5,9},{9,13},{2,6},{6,10},{10,14},{3,7},{... | collective-permute-start | bytes 2654216 | tf_op jit(solution)/shard_map/ppermute | solution.py:16
  103.7 1.4 collective-permute-start
  105.1 2.1 concatenate.11
  107.1 1.3 collective-permute-start.12
  108.4 1.7 constant_dynamic-update-slice_fusion.17
  110.1 1.3 collective-permute-start.13
  111.4 1.7 constant_dynamic-update-slice_fusion.8
  113.1 7.6 %collective-permute-start.1 = (bf16[1152,384]{1,0:T(8,128)(2,1)S(1)}, bf16[1152,384]{1,0:T(8,128)(2,1)S(1)}, u32[]{:S(2)}, u32[]{:S(2)}) collective-permute-start(bf16[1152,384]{1,0:T(8,128)(2,1)S(1)} %bitcast.59), channel_id=1, source_target_pairs={{0,12},{1,13},{2,14},{3,15},{16,28},{17,29},{18,30},{19,31}} | collective-permute-start | bytes 2654216 | tf_op jit(solution)/shard_map/ppermute | solution.py:16
  120.7 1.1 constant_dynamic-update-slice_fusion.16
  121.8 1.5 collective-permute-start.2
  123.3 1.1 constant_dynamic-update-slice_fusion.15
  124.4 2.6 collective-permute-start.3
  127.0 2.2 constant_dynamic-update-slice_fusion.14
  130.1 10.6 %collective-permute-done.1 = bf16[1152,384]{1,0:T(8,128)(2,1)S(1)} collective-permute-done((bf16[1152,384]{1,0:T(8,128)(2,1)S(1)}, bf16[1152,384]{1,0:T(8,128)(2,1)S(1)}, u32[]{:S(2)}, u32[]{:S(2)}) %collective-permute-start.1) | collective-permute-done | bytes 884768 | tf_op jit(solution)/shard_map/ppermute | solution.py:16
  140.8 1.3 collective-permute-start.14
  143.1 16.6 %collective-permute-done.2 = bf16[1152,384]{1,0:T(8,128)(2,1)S(1)} collective-permute-done((bf16[1152,384]{1,0:T(8,128)(2,1)S(1)}, bf16[1152,384]{1,0:T(8,128)(2,1)S(1)}, u32[]{:S(2)}, u32[]{:S(2)}) %collective-permute-start.2) | collective-permute-done | bytes 884768 | tf_op jit(solution)/shard_map/ppermute | solution.py:16
  159.7 1.3 collective-permute-start.4
  162.0 15.1 %collective-permute-done.3 = bf16[1152,384]{1,0:T(8,128)(2,1)S(1)} collective-permute-done((bf16[1152,384]{1,0:T(8,128)(2,1)S(1)}, bf16[1152,384]{1,0:T(8,128)(2,1)S(1)}, u32[]{:S(2)}, u32[]{:S(2)}) %collective-permute-start.3) | collective-permute-done | bytes 884768 | tf_op jit(solution)/shard_map/ppermute | solution.py:16
  177.1 1.3 collective-permute-start.5
  180.4 1.3 collective-permute-start.6
  182.7 4.3 %collective-permute-done.13 = bf16[1152,384]{1,0:T(8,128)(2,1)S(1)} collective-permute-done((bf16[1152,384]{1,0:T(8,128)(2,1)S(1)}, bf16[1152,384]{1,0:T(8,128)(2,1)S(1)}, u32[]{:S(2)}, u32[]{:S(2)}) %collective-permute-start.13) | collective-permute-done | bytes 884768 | tf_op jit(solution)/shard_map/ppermute | solution.py:16
  190.4 13.4 %collective-permute-done.4 = bf16[1152,384]{1,0:T(8,128)(2,1)S(1)} collective-permute-done((bf16[1152,384]{1,0:T(8,128)(2,1)S(1)}, bf16[1152,384]{1,0:T(8,128)(2,1)S(1)}, u32[]{:S(2)}, u32[]{:S(2)}) %collective-permute-start.4) | collective-permute-done | bytes 884768 | tf_op jit(solution)/shard_map/ppermute | solution.py:16
  204.8 55.9 %collective-permute-done.5 = bf16[1152,384]{1,0:T(8,128)(2,1)S(1)} collective-permute-done((bf16[1152,384]{1,0:T(8,128)(2,1)S(1)}, bf16[1152,384]{1,0:T(8,128)(2,1)S(1)}, u32[]{:S(2)}, u32[]{:S(2)}) %collective-permute-start.5) | collective-permute-done | bytes 884768 | tf_op jit(solution)/shard_map/ppermute | solution.py:16
  260.7 1.1 constant_dynamic-update-slice_fusion.2
  264.3 76.2 %while.27 = (s32[]{:T(128)}, bf16[3,384,384]{2,1,0:T(8,128)(2,1)}, s32[3]{0:T(128)S(1)}, bf16[3,384,384]{2,1,0:T(8,128)(2,1)}, s32[3,8]{1,0:T(4,128)S(1)}, /*ind...) while((s32[]{:T(128)}, bf16[3,384,384]{2,1,0:T(8,128)(2,1)}, ...), condition=%wide.region_5.6_spmd.clone, body=%wide.region_0.5_spmd.clone.sunk | while | flops 612344704 | bytes 26889600 | solution.py:86
  267.5 4.0 %gather_fusion.1 = bf16[8,384,384]{2,1,0:T(8,128)(2,1)S(1)} fusion(bf16[23,384,384]{2,1,0:T(8,128)(2,1)} %get-tuple-element.422, s32[1024]{0:T(1024)S(1)} %pad_clamp_fusion.2), kind=kCustom, calls=%fused_computation.1.clone.clone.1 | custom fusion | bytes 4718624 | tf_op jit(solution)/shard_map/while/body/eval_jaxpr/gather | solution.py:62
  271.5 5.2 %gather_fusion.2 = bf16[8,384,384]{2,1,0:T(8,128)(2,1)} fusion(bf16[23,384,384]{2,1,0:T(8,128)(2,1)} %get-tuple-element.423, s32[1024]{0:T(1024)S(1)} %pad_clamp_fusion.2), kind=kCustom, calls=%fused_computation.2.clone.clone.1 | custom fusion | bytes 4718624 | tf_op jit(solution)/shard_map/while/body/eval_jaxpr/gather | solution.py:63
  277.7 11.2 %while.28 = (s32[]{:T(128)}, bf16[384,384]{1,0:T(8,128)(2,1)S(1)}, pred[8,384]{1,0:T(8,128)(4,1)}, bf16[384,384]{1,0:T(8,128)(2,1)S(1)}, bf16[3072,384]{1,0:T(8,...) while((s32[]{:T(128)}, bf16[384,384]{1,0:T(8,128)(2,1)S(1)}, ...), condition=%wide.wide.region_4.4_spmd, body=%wide.wide.region_1.3_spmd.sunk | while | flops 612334848 | bytes 15939227 | solution.py:84
  279.4 2.0 fusion.43
  283.2 2.0 fusion.43
  286.9 2.0 fusion.43
  292.9 4.0 %gather_fusion.1 = bf16[8,384,384]{2,1,0:T(8,128)(2,1)S(1)} fusion(bf16[23,384,384]{2,1,0:T(8,128)(2,1)} %get-tuple-element.422, s32[1024]{0:T(1024)S(1)} %pad_clamp_fusion.2), kind=kCustom, calls=%fused_computation.1.clone.clone.1 | custom fusion | bytes 4718624 | tf_op jit(solution)/shard_map/while/body/eval_jaxpr/gather | solution.py:62
  296.8 5.2 %gather_fusion.2 = bf16[8,384,384]{2,1,0:T(8,128)(2,1)} fusion(bf16[23,384,384]{2,1,0:T(8,128)(2,1)} %get-tuple-element.423, s32[1024]{0:T(1024)S(1)} %pad_clamp_fusion.2), kind=kCustom, calls=%fused_computation.2.clone.clone.1 | custom fusion | bytes 4718624 | tf_op jit(solution)/shard_map/while/body/eval_jaxpr/gather | solution.py:63
  303.1 11.2 %while.28 = (s32[]{:T(128)}, bf16[384,384]{1,0:T(8,128)(2,1)S(1)}, pred[8,384]{1,0:T(8,128)(4,1)}, bf16[384,384]{1,0:T(8,128)(2,1)S(1)}, bf16[3072,384]{1,0:T(8,...) while((s32[]{:T(128)}, bf16[384,384]{1,0:T(8,128)(2,1)S(1)}, ...), condition=%wide.wide.region_4.4_spmd, body=%wide.wide.region_1.3_spmd.sunk | while | flops 612334848 | bytes 15939227 | solution.py:84
  304.8 2.0 fusion.43
  308.5 2.0 fusion.43
  312.3 2.0 fusion.43
  318.2 4.0 %gather_fusion.1 = bf16[8,384,384]{2,1,0:T(8,128)(2,1)S(1)} fusion(bf16[23,384,384]{2,1,0:T(8,128)(2,1)} %get-tuple-element.422, s32[1024]{0:T(1024)S(1)} %pad_clamp_fusion.2), kind=kCustom, calls=%fused_computation.1.clone.clone.1 | custom fusion | bytes 4718624 | tf_op jit(solution)/shard_map/while/body/eval_jaxpr/gather | solution.py:62
  322.2 5.2 %gather_fusion.2 = bf16[8,384,384]{2,1,0:T(8,128)(2,1)} fusion(bf16[23,384,384]{2,1,0:T(8,128)(2,1)} %get-tuple-element.423, s32[1024]{0:T(1024)S(1)} %pad_clamp_fusion.2), kind=kCustom, calls=%fused_computation.2.clone.clone.1 | custom fusion | bytes 4718624 | tf_op jit(solution)/shard_map/while/body/eval_jaxpr/gather | solution.py:63
  328.5 11.2 %while.28 = (s32[]{:T(128)}, bf16[384,384]{1,0:T(8,128)(2,1)S(1)}, pred[8,384]{1,0:T(8,128)(4,1)}, bf16[384,384]{1,0:T(8,128)(2,1)S(1)}, bf16[3072,384]{1,0:T(8,...) while((s32[]{:T(128)}, bf16[384,384]{1,0:T(8,128)(2,1)S(1)}, ...), condition=%wide.wide.region_4.4_spmd, body=%wide.wide.region_1.3_spmd.sunk | while | flops 612334848 | bytes 15939227 | solution.py:84
  330.2 2.0 fusion.43
  333.9 2.0 fusion.43
  337.7 2.0 fusion.43
  340.5 16.1 %all_to_all.73 = bf16[4,288,384]{2,1,0:T(8,128)(2,1)S(1)} all-to-all(bf16[4,288,384]{2,1,0:T(8,128)(2,1)} %bitcast.78), channel_id=1, replica_groups=mesh['clips'=2,'ctx'=4,'head'=4] {'head'}, dimensions={0} | all-to-all | bytes 1769472 | tf_op jit(solution)/shard_map/all_to_all | solution.py:88
  (110 shorter events, 42.3 us)
Async XLA Ops:
  0.0 22.7 %copy-start.4 = (s32[3]{0:T(128)S(1)}, s32[3]{0:T(128)}, u32[]{:S(2)}) copy-start(s32[3]{0:T(128)} %param.13) | copy-start | bytes 40
  0.0 30.7 %copy-start = (bf16[288,1536]{1,0:T(8,128)(2,1)S(1)}, bf16[288,1536]{1,0:T(8,128)(2,1)}, u32[]{:S(2)}) copy-start(bf16[288,1536]{1,0:T(8,128)(2,1)} %param.9) | copy-start | bytes 2654212
  0.0 105.1 %copy-start.5 = (s32[3,8]{1,0:T(4,128)S(1)}, s32[3,8]{1,0:T(4,128)}, u32[]{:S(2)}) copy-start(s32[3,8]{1,0:T(4,128)} %param.12) | copy-start | bytes 292
  2.3 16.9 %all-to-all-start.2 = ((bf16[288,4,384]{2,0,1:T(8,128)(2,1)}), bf16[288,4,384]{2,0,1:T(8,128)(2,1)S(1)}, u32[]{:S(2)}, u32[]{:S(2)}) async-start(bf16[288,4,384]{2,0,1:T(8,128)(2,1)} %bitcast.39), calls=%async_computation.2 | async-start | bytes 1769472 | tf_op jit(solution)/shard_map/all_to_all | solution.py:29
  19.2 17.5 %all-to-all-start.1 = ((bf16[288,4,384]{2,0,1:T(8,128)(2,1)}), bf16[288,4,384]{2,0,1:T(8,128)(2,1)S(1)}, u32[]{:S(2)}, u32[]{:S(2)}) async-start(bf16[288,4,384]{2,0,1:T(8,128)(2,1)} %bitcast.40), calls=%async_computation.1 | async-start | bytes 1769472 | tf_op jit(solution)/shard_map/all_to_all | solution.py:28
  22.7 24.2 %collective-permute-start.17 = (s32[3]{0:T(128)S(1)}, s32[3]{0:T(128)S(1)}, u32[]{:S(2)}, u32[]{:S(2)}) collective-permute-start(s32[3]{0:T(128)S(1)} %copy-done.4), channel_id=1, source_target_pairs={{0,12},{1,13},{2,14},{3,15},{16,28},{17,29},{18,30},{19,31}} | collective-permute-start | bytes 44 | tf_op jit(solution)/shard_map/ppermute | solution.py:16
  29.5 12.3 %collective-permute-start.16 = (s32[1]{0:T(128)}, s32[1]{0:T(128)}, u32[]{:S(2)}, u32[]{:S(2)}) collective-permute-start(s32[1]{0:T(128)} %get-tuple-element.212), channel_id=1, source_target_pairs={} | collective-permute-start | bytes 20 | tf_op jit(solution)/shard_map/ppermute | solution.py:16
  31.8 81.4 %collective-permute-start.9 = (bf16[1152,384]{1,0:T(8,128)(2,1)S(1)}, bf16[1152,384]{1,0:T(8,128)(2,1)S(1)}, u32[]{:S(2)}, u32[]{:S(2)}) collective-permute-start(bf16[1152,384]{1,0:T(8,128)(2,1)S(1)} %bitcast.66), channel_id=1, source_target_pairs={{0,12},{1,13},{2,14},{3,15},{16,28},{17,29},{18,30},{19,31}} | collective-permute-start | bytes 2654216 | tf_op jit(solution)/shard_map/ppermute | solution.py:16
  33.1 88.7 %collective-permute-start.10 = (bf16[1152,384]{1,0:T(8,128)(2,1)S(1)}, bf16[1152,384]{1,0:T(8,128)(2,1)S(1)}, u32[]{:S(2)}, u32[]{:S(2)}) collective-permute-start(bf16[1152,384]{1,0:T(8,128)(2,1)S(1)} %bitcast.67), channel_id=1, source_target_pairs={{0,8},{4,12},{1,9},{5,13},{2,10},{6,14},{3,11},{7,15},{16,24},{20,... | collective-permute-start | bytes 2654216 | tf_op jit(solution)/shard_map/ppermute | solution.py:16
  35.3 71.8 %collective-permute-start.8 = (bf16[384,384]{1,0:T(8,128)(2,1)}, bf16[384,384]{1,0:T(8,128)(2,1)}, u32[]{:S(2)}, u32[]{:S(2)}) collective-permute-start(bf16[384,384]{1,0:T(8,128)(2,1)} %get-tuple-element.208), channel_id=1, source_target_pairs={} | collective-permute-start | bytes 884744 | tf_op jit(solution)/shard_map/ppermute | solution.py:16
  36.7 227.6 %all-to-all-start = ((bf16[288,4,384]{2,0,1:T(8,128)(2,1)}), bf16[288,4,384]{2,0,1:T(8,128)(2,1)}, u32[]{:S(2)}, u32[]{:S(2)}) async-start(bf16[288,4,384]{2,0,1:T(8,128)(2,1)} %bitcast.41), calls=%async_computation | async-start | bytes 1769472 | tf_op jit(solution)/shard_map/all_to_all | solution.py:27
  41.9 1.2 collective-permute-start.23
  43.1 28.5 %collective-permute-start.18 = (s32[3]{0:T(128)S(1)}, s32[3]{0:T(128)S(1)}, u32[]{:S(2)}, u32[]{:S(2)}) collective-permute-start(s32[3]{0:T(128)S(1)} %copy-done.4), channel_id=1, source_target_pairs={{0,8},{4,12},{1,9},{5,13},{2,10},{6,14},{3,11},{7,15},{16,24},{20,... | collective-permute-start | bytes 44 | tf_op jit(solution)/shard_map/ppermute | solution.py:16
  46.9 26.0 %collective-permute-start.19 = (s32[3]{0:T(128)S(1)}, s32[3]{0:T(128)S(1)}, u32[]{:S(2)}, u32[]{:S(2)}) collective-permute-start(s32[3]{0:T(128)S(1)} %copy-done.4), channel_id=1, source_target_pairs={{0,4},{4,8},{8,12},{1,5},{5,9},{9,13},{2,6},{6,10},{10,14},{3,7},{... | collective-permute-start | bytes 44 | tf_op jit(solution)/shard_map/ppermute | solution.py:16
  71.6 31.6 %copy-start.6 = (s32[3]{0:T(128)}, s32[3]{0:T(128)S(1)}, u32[]{:S(2)}) copy-start(s32[3]{0:T(128)S(1)} %collective-permute-done.18) | copy-start | bytes 40
  71.6 23.9 %collective-permute-start.20 = (s32[3]{0:T(128)S(1)}, s32[3]{0:T(128)S(1)}, u32[]{:S(2)}, u32[]{:S(2)}) collective-permute-start(s32[3]{0:T(128)S(1)} %copy-done.4), channel_id=1, source_target_pairs={{4,0},{8,4},{12,8},{5,1},{9,5},{13,9},{6,2},{10,6},{14,10},{7,3},{... | collective-permute-start | bytes 44 | tf_op jit(solution)/shard_map/ppermute | solution.py:16
  72.9 30.3 %copy-start.7 = (s32[3]{0:T(128)}, s32[3]{0:T(128)S(1)}, u32[]{:S(2)}) copy-start(s32[3]{0:T(128)S(1)} %collective-permute-done.19) | copy-start | bytes 40
  72.9 25.3 %collective-permute-start.21 = (s32[3]{0:T(128)S(1)}, s32[3]{0:T(128)S(1)}, u32[]{:S(2)}, u32[]{:S(2)}) collective-permute-start(s32[3]{0:T(128)S(1)} %copy-done.4), channel_id=1, source_target_pairs={{8,0},{12,4},{9,1},{13,5},{10,2},{14,6},{11,3},{15,7},{24,16},{28,... | collective-permute-start | bytes 44 | tf_op jit(solution)/shard_map/ppermute | solution.py:16
  95.5 7.7 %copy-start.8 = (s32[3]{0:T(128)}, s32[3]{0:T(128)S(1)}, u32[]{:S(2)}) copy-start(s32[3]{0:T(128)S(1)} %collective-permute-done.20) | copy-start | bytes 40
  95.5 7.7 %collective-permute-start.22 = (s32[3]{0:T(128)S(1)}, s32[3]{0:T(128)S(1)}, u32[]{:S(2)}, u32[]{:S(2)}) collective-permute-start(s32[3]{0:T(128)S(1)} %copy-done.4), channel_id=1, source_target_pairs={{12,0},{13,1},{14,2},{15,3},{28,16},{29,17},{30,18},{31,19}} | collective-permute-start | bytes 44 | tf_op jit(solution)/shard_map/ppermute | solution.py:16
  98.2 5.0 %copy-start.9 = (s32[3]{0:T(128)}, s32[3]{0:T(128)S(1)}, u32[]{:S(2)}) copy-start(s32[3]{0:T(128)S(1)} %collective-permute-done.21) | copy-start | bytes 40
  98.2 26.1 %collective-permute-start.11 = (bf16[1152,384]{1,0:T(8,128)(2,1)S(1)}, bf16[1152,384]{1,0:T(8,128)(2,1)}, u32[]{:S(2)}, u32[]{:S(2)}) collective-permute-start(bf16[1152,384]{1,0:T(8,128)(2,1)S(1)} %bitcast.69), channel_id=1, source_target_pairs={{0,4},{4,8},{8,12},{1,5},{5,9},{9,13},{2,6},{6,10},{10,14},{3,7},{... | collective-permute-start | bytes 2654216 | tf_op jit(solution)/shard_map/ppermute | solution.py:16
  103.2 0.5 copy-start.10
  103.7 6.4 %collective-permute-start = (bf16[384,384]{1,0:T(8,128)(2,1)}, bf16[384,384]{1,0:T(8,128)(2,1)}, u32[]{:S(2)}, u32[]{:S(2)}) collective-permute-start(bf16[384,384]{1,0:T(8,128)(2,1)} %get-tuple-element.210), channel_id=1, source_target_pairs={} | collective-permute-start | bytes 884744 | tf_op jit(solution)/shard_map/ppermute | solution.py:16
  107.1 73.3 %collective-permute-start.12 = (bf16[1152,384]{1,0:T(8,128)(2,1)S(1)}, bf16[1152,384]{1,0:T(8,128)(2,1)S(1)}, u32[]{:S(2)}, u32[]{:S(2)}) collective-permute-start(bf16[1152,384]{1,0:T(8,128)(2,1)S(1)} %bitcast.70), channel_id=1, source_target_pairs={{4,0},{8,4},{12,8},{5,1},{9,5},{13,9},{6,2},{10,6},{14,10},{7,3},{... | collective-permute-start | bytes 2654216 | tf_op jit(solution)/shard_map/ppermute | solution.py:16
  110.1 76.9 %collective-permute-start.13 = (bf16[1152,384]{1,0:T(8,128)(2,1)S(1)}, bf16[1152,384]{1,0:T(8,128)(2,1)S(1)}, u32[]{:S(2)}, u32[]{:S(2)}) collective-permute-start(bf16[1152,384]{1,0:T(8,128)(2,1)S(1)} %bitcast.71), channel_id=1, source_target_pairs={{8,0},{12,4},{9,1},{13,5},{10,2},{14,6},{11,3},{15,7},{24,16},{28,... | collective-permute-start | bytes 2654216 | tf_op jit(solution)/shard_map/ppermute | solution.py:16
  113.1 27.6 %collective-permute-start.1 = (bf16[1152,384]{1,0:T(8,128)(2,1)S(1)}, bf16[1152,384]{1,0:T(8,128)(2,1)S(1)}, u32[]{:S(2)}, u32[]{:S(2)}) collective-permute-start(bf16[1152,384]{1,0:T(8,128)(2,1)S(1)} %bitcast.59), channel_id=1, source_target_pairs={{0,12},{1,13},{2,14},{3,15},{16,28},{17,29},{18,30},{19,31}} | collective-permute-start | bytes 2654216 | tf_op jit(solution)/shard_map/ppermute | solution.py:16
  121.8 65.2 %copy-start.2 = (bf16[384,384]{1,0:T(8,128)(2,1)S(1)}, bf16[384,384]{1,0:T(8,128)(2,1)}, u32[]{:S(2)}) copy-start(bf16[384,384]{1,0:T(8,128)(2,1)} %get-tuple-element.207) | copy-start | bytes 884740
  121.8 37.9 %collective-permute-start.2 = (bf16[1152,384]{1,0:T(8,128)(2,1)S(1)}, bf16[1152,384]{1,0:T(8,128)(2,1)S(1)}, u32[]{:S(2)}, u32[]{:S(2)}) collective-permute-start(bf16[1152,384]{1,0:T(8,128)(2,1)S(1)} %bitcast.60), channel_id=1, source_target_pairs={{0,8},{4,12},{1,9},{5,13},{2,10},{6,14},{3,11},{7,15},{16,24},{20,... | collective-permute-start | bytes 2654216 | tf_op jit(solution)/shard_map/ppermute | solution.py:16
  124.4 64.3 %copy-start.3 = (bf16[384,384]{1,0:T(8,128)(2,1)S(1)}, bf16[384,384]{1,0:T(8,128)(2,1)}, u32[]{:S(2)}) copy-start(bf16[384,384]{1,0:T(8,128)(2,1)} %get-tuple-element.209) | copy-start | bytes 884740
  124.4 52.7 %collective-permute-start.3 = (bf16[1152,384]{1,0:T(8,128)(2,1)S(1)}, bf16[1152,384]{1,0:T(8,128)(2,1)S(1)}, u32[]{:S(2)}, u32[]{:S(2)}) collective-permute-start(bf16[1152,384]{1,0:T(8,128)(2,1)S(1)} %bitcast.61), channel_id=1, source_target_pairs={{0,4},{4,8},{8,12},{1,5},{5,9},{9,13},{2,6},{6,10},{10,14},{3,7},{... | collective-permute-start | bytes 2654216 | tf_op jit(solution)/shard_map/ppermute | solution.py:16
  140.8 47.9 %collective-permute-start.14 = (bf16[1152,384]{1,0:T(8,128)(2,1)S(1)}, bf16[1152,384]{1,0:T(8,128)(2,1)S(1)}, u32[]{:S(2)}, u32[]{:S(2)}) collective-permute-start(bf16[1152,384]{1,0:T(8,128)(2,1)S(1)} %bitcast.73), channel_id=1, source_target_pairs={{12,0},{13,1},{14,2},{15,3},{28,16},{29,17},{30,18},{31,19}} | collective-permute-start | bytes 2654216 | tf_op jit(solution)/shard_map/ppermute | solution.py:16
  159.7 44.1 %collective-permute-start.4 = (bf16[1152,384]{1,0:T(8,128)(2,1)S(1)}, bf16[1152,384]{1,0:T(8,128)(2,1)S(1)}, u32[]{:S(2)}, u32[]{:S(2)}) collective-permute-start(bf16[1152,384]{1,0:T(8,128)(2,1)S(1)} %bitcast.62), channel_id=1, source_target_pairs={{4,0},{8,4},{12,8},{5,1},{9,5},{13,9},{6,2},{10,6},{14,10},{7,3},{... | collective-permute-start | bytes 2654216 | tf_op jit(solution)/shard_map/ppermute | solution.py:16
  177.1 83.6 %collective-permute-start.5 = (bf16[1152,384]{1,0:T(8,128)(2,1)S(1)}, bf16[1152,384]{1,0:T(8,128)(2,1)S(1)}, u32[]{:S(2)}, u32[]{:S(2)}) collective-permute-start(bf16[1152,384]{1,0:T(8,128)(2,1)S(1)} %bitcast.63), channel_id=1, source_target_pairs={{8,0},{12,4},{9,1},{13,5},{10,2},{14,6},{11,3},{15,7},{24,16},{28,... | collective-permute-start | bytes 2654216 | tf_op jit(solution)/shard_map/ppermute | solution.py:16
  180.4 82.1 %collective-permute-start.6 = (bf16[1152,384]{1,0:T(8,128)(2,1)S(1)}, bf16[1152,384]{1,0:T(8,128)(2,1)S(1)}, u32[]{:S(2)}, u32[]{:S(2)}) collective-permute-start(bf16[1152,384]{1,0:T(8,128)(2,1)S(1)} %bitcast.65), channel_id=1, source_target_pairs={{12,0},{13,1},{14,2},{15,3},{28,16},{29,17},{30,18},{31,19}} | collective-permute-start | bytes 2654216 | tf_op jit(solution)/shard_map/ppermute | solution.py:16
  187.0 74.8 %collective-permute-start.15 = (bf16[384,384]{1,0:T(8,128)(2,1)S(1)}, bf16[384,384]{1,0:T(8,128)(2,1)S(1)}, u32[]{:S(2)}, u32[]{:S(2)}) collective-permute-start(bf16[384,384]{1,0:T(8,128)(2,1)S(1)} %copy-done.2), channel_id=1, source_target_pairs={} | collective-permute-start | bytes 884744 | tf_op jit(solution)/shard_map/ppermute | solution.py:16
  188.7 74.9 %collective-permute-start.7 = (bf16[384,384]{1,0:T(8,128)(2,1)S(1)}, bf16[384,384]{1,0:T(8,128)(2,1)S(1)}, u32[]{:S(2)}, u32[]{:S(2)}) collective-permute-start(bf16[384,384]{1,0:T(8,128)(2,1)S(1)} %copy-done.3), channel_id=1, source_target_pairs={} | collective-permute-start | bytes 884744 | tf_op jit(solution)/shard_map/ppermute | solution.py:16
  267.4 10.3 %copy-start.1 = (pred[8,384]{1,0:T(8,128)(4,1)}, pred[8,384]{1,0:T(8,128)(4,1)S(1)}, u32[]{:S(2)}) copy-start(pred[8,384]{1,0:T(8,128)(4,1)S(1)} %gather_fusion) | copy-start | bytes 9220 | tf_op jit(solution)/shard_map/while
  292.8 10.3 %copy-start.1 = (pred[8,384]{1,0:T(8,128)(4,1)}, pred[8,384]{1,0:T(8,128)(4,1)S(1)}, u32[]{:S(2)}) copy-start(pred[8,384]{1,0:T(8,128)(4,1)S(1)} %gather_fusion) | copy-start | bytes 9220 | tf_op jit(solution)/shard_map/while
  318.2 10.3 %copy-start.1 = (pred[8,384]{1,0:T(8,128)(4,1)}, pred[8,384]{1,0:T(8,128)(4,1)S(1)}, u32[]{:S(2)}) copy-start(pred[8,384]{1,0:T(8,128)(4,1)S(1)} %gather_fusion) | copy-start | bytes 9220 | tf_op jit(solution)/shard_map/while
where the time goes:
time: 359 us; the launch traced here: 358 us
  waiting for transfers between devices  170 us (47%)
  local copies, waits for them, and re-layouts  68.2 us (19%)
  starting transfers between devices  62.8 us (17%)
  matrix products  26.5 us (7%)
  blocking collectives  16.1 us (4%)
  other arithmetic  7.3 us (2%)
  loops' own time  5.99 us (2%)
    ppermute x24, waiting for transfers between devices, shifted(): return lax.ppermute(array, axis, pairs)  160 us
    ppermute x24, starting transfers between devices, shifted(): return lax.ppermute(array, axis, pairs)  50.8 us
    unnamed x36, local copies, waits for them, and re-layouts  19.4 us
    dot_general x9, matrix products, one_head(): summed = jnp.dot(rounded, value_rows, preferred_element_type=jnp.float32)  18.2 us
    all_to_all x1, blocking collectives, shards(): lax.all_to_all(outputs, 'head', split_axis=0, concat_axis=1, tiled=True)  16.1 us
    gather x3, local copies, waits for them, and re-layouts, one_tile(): value_block = ext_values[listed].reshape(NB * TILE, local_width)  15.6 us
    gather x3, local copies, waits for them, and re-layouts, one_tile(): key_block = ext_keys[listed].reshape(NB * TILE, local_width)  12 us
    all_to_all x1, waiting for transfers between devices, shards(): lax.all_to_all(values, 'head', split_axis=1, concat_axis=0, tiled=True)  10.5 us
  transfers between devices with their start and end apart: 27, of which 10 were waited for; matrix products, arithmetic and copies ran while one was open for 8% of the time, Pallas kernels for 0%

commit v1 on v0

--- a/solution.py
+++ b/solution.py
@@ -8,6 +8,22 @@
 NB = 8
 REACH = 10
 HOPS = 4
+
+
+def exchange_in_pairs(array, axis, split, join):
+    ways, here = (lax.axis_size(axis), lax.axis_index(axis))
+    width = array.shape[split] // ways
+    dims = list(array.shape)
+    dims[split] = width
+    height = dims[join]
+    dims[join] = height * ways
+    full = jnp.zeros(dims, array.dtype)
+    for mask in range(ways):
+        part = lax.dynamic_slice_in_dim(array, (here ^ mask) * width, width, axis=split)
+        if mask:
+            part = lax.ppermute(part, axis, [(d, d ^ mask) for d in range(ways)])
+        full = lax.dynamic_update_slice_in_dim(full, part, (here ^ mask) * height, axis=join)
+    return full
 
 
 def shifted(array, axis, by):
@@ -26,7 +42,7 @@
     block_queries, block_keys, block_values = (
         lax.all_to_all(queries, "head", split_axis=1, concat_axis=0, tiled=True),
         lax.all_to_all(keys, "head", split_axis=1, concat_axis=0, tiled=True),
-        lax.all_to_all(values, "head", split_axis=1, concat_axis=0, tiled=True),
+        exchange_in_pairs(values, "head", 1, 0),
     )
     tiles_here = tile_counts.shape[0]
     local_width = block_queries.shape[1]

time: 359 us -> 353 us (0.983)
  waiting for transfers between devices: 170 us -> 131 us
  starting transfers between devices: 62.8 us -> 94.6 us
    ppermute x24, starting transfers between devices: 50.8 us -> 83.6 us  [shifted(): return lax.ppermute(array, axis, pairs)]
    ppermute x24, waiting for transfers between devices: 160 us -> 131 us  [shifted(): return lax.ppermute(array, axis, pairs)]
    all_to_all x1 -> x0, waiting for transfers between devices: 10.5 us -> none  [shards(): lax.all_to_all(values, 'head', split_axis=1, concat_axis=0, tiled=True)]
    all_to_all x1 -> x0, starting transfers between devices: 4.24 us -> none  [shards(): lax.all_to_all(values, 'head', split_axis=1, concat_axis=0, tiled=True)]
    unnamed x36 -> x34, local copies, waits for them, and re-layouts: 19.4 us -> 19.5 us
  transfers between devices with their start and end apart: 27 -> 29, of which waited for: 10 -> 9; matrix products, arithmetic and copies ran while one was open for 8% -> 9% of each run, Pallas kernels for 0% -> 0%
where the time goes in v1:
time: 353 us; the launch traced here: 351 us
  waiting for transfers between devices  131 us (37%)
  starting transfers between devices  94.6 us (27%)
  local copies, waits for them, and re-layouts  70.1 us (20%)
  matrix products  26.5 us (8%)
  blocking collectives  16.1 us (5%)
  other arithmetic  7.3 us (2%)
  loops' own time  5.92 us (2%)
    ppermute x24, waiting for transfers between devices, shifted(): return lax.ppermute(array, axis, pairs)  131 us
    ppermute x24, starting transfers between devices, shifted(): return lax.ppermute(array, axis, pairs)  83.6 us
    unnamed x34, local copies, waits for them, and re-layouts  19.5 us
    dot_general x9, matrix products, one_head(): summed = jnp.dot(rounded, value_rows, preferred_element_type=jnp.float32)  18.3 us
    all_to_all x1, blocking collectives, shards(): lax.all_to_all(outputs, 'head', split_axis=0, concat_axis=1, tiled=True)  16.1 us
    gather x3, local copies, waits for them, and re-layouts, one_tile(): value_block = ext_values[listed].reshape(NB * TILE, local_width)  15.6 us
    gather x3, local copies, waits for them, and re-layouts, one_tile(): key_block = ext_keys[listed].reshape(NB * TILE, local_width)  12 us
    dot_general x9, matrix products, one_head(): lax.dot_general(query_rows, key_rows, (((1,), (1,)), ((), ())), preferred...  8.23 us
  transfers between devices with their start and end apart: 29, of which 9 were waited for; matrix products, arithmetic and copies ran while one was open for 9% of the time, Pallas kernels for 0%

profile of v1, /device:TPU:0, one launch (start us, length us, event | category | flops | bytes accessed | tf_op | source)
XLA Modules:
  0.0 351.4 jit_solution(7729267410968066943)
XLA Ops:
  0.1 1.5 constant_dynamic-slice_fusion.1
  2.1 2.6 collective-permute-start.9
  4.7 2.2 copy.18
  6.9 3.5 all-to-all-start.1
  10.4 5.8 %collective-permute-start.20 = (s32[3]{0:T(128)}, s32[3]{0:T(128)S(1)}, u32[]{:S(2)}, u32[]{:S(2)}) collective-permute-start(s32[3]{0:T(128)} %param.13), channel_id=1, source_target_pairs={{0,12},{1,13},{2,14},{3,15},{16,28},{17,29},{18,30},{19,31}} | collective-permute-start | bytes 44 | tf_op jit(solution)/shard_map/ppermute | solution.py:32
  16.2 1.3 fusion.26
  17.5 1.2 collective-permute-start.19
  21.7 1.4 collective-permute-start.12
  23.1 1.3 collective-permute-start.13
  25.3 1.4 collective-permute-start.11
  26.6 4.2 %all-to-all-start = ((bf16[288,4,384]{2,0,1:T(8,128)(2,1)}), bf16[288,4,384]{2,0,1:T(8,128)(2,1)}, u32[]{:S(2)}, u32[]{:S(2)}) async-start(bf16[288,4,384]{2,0,1:T(8,128)(2,1)} %bitcast.34), calls=%async_computation | async-start | bytes 1769472 | tf_op jit(solution)/shard_map/all_to_all | solution.py:43
  31.8 1.1 collective-permute-start.26
  32.9 3.0 collective-permute-start.21
  36.0 3.5 collective-permute-start.22
  39.4 22.1 %collective-permute-done.21 = s32[3]{0:T(128)S(1)} collective-permute-done((s32[3]{0:T(128)S(1)}, s32[3]{0:T(128)S(1)}, u32[]{:S(2)}, u32[]{:S(2)}) %collective-permute-start.21) | collective-permute-done | bytes 44 | tf_op jit(solution)/shard_map/ppermute | solution.py:32
  61.6 1.3 collective-permute-start.23
  62.9 1.3 collective-permute-start.24
  64.2 21.3 %collective-permute-done.23 = s32[3]{0:T(128)S(1)} collective-permute-done((s32[3]{0:T(128)S(1)}, s32[3]{0:T(128)S(1)}, u32[]{:S(2)}, u32[]{:S(2)}) %collective-permute-start.23) | collective-permute-done | bytes 44 | tf_op jit(solution)/shard_map/ppermute | solution.py:32
  85.4 1.3 collective-permute-start.25
  86.7 1.5 collective-permute-done.24
  88.2 4.9 %collective-permute-start.14 = (bf16[1152,384]{1,0:T(8,128)(2,1)S(1)}, bf16[1152,384]{1,0:T(8,128)(2,1)}, u32[]{:S(2)}, u32[]{:S(2)}) collective-permute-start(bf16[1152,384]{1,0:T(8,128)(2,1)S(1)} %constant_dynamic-update-slice_fusion.18), channel_id=1, source_target_pairs={{0,4},{4,8},{8,12},{1,5},{5,9},{9,13},{2,6},{6,10},{10,14},{3,7},{... | collective-permute-start | bytes 2654216 | tf_op jit(solution)/shard_map/ppermute | solution.py:32
  93.7 1.4 collective-permute-start
  95.1 1.9 concatenate.11
  97.0 1.3 collective-permute-start.15
  98.3 1.7 constant_dynamic-update-slice_fusion.17
  100.0 1.3 collective-permute-start.16
  101.3 1.7 constant_dynamic-update-slice_fusion.8
  103.0 1.3 collective-permute-start.17
  104.3 1.1 constant_dynamic-update-slice_fusion.16
  106.2 1.1 constant_dynamic-update-slice_fusion.15
  107.2 2.9 collective-permute-done.14
  110.1 5.4 %collective-permute-start.1 = (bf16[1152,384]{1,0:T(8,128)(2,1)S(1)}, bf16[1152,384]{1,0:T(8,128)(2,1)S(1)}, u32[]{:S(2)}, u32[]{:S(2)}) collective-permute-start(bf16[1152,384]{1,0:T(8,128)(2,1)S(1)} %bitcast.52), channel_id=1, source_target_pairs={{0,12},{1,13},{2,14},{3,15},{16,28},{17,29},{18,30},{19,31}} | collective-permute-start | bytes 2654216 | tf_op jit(solution)/shard_map/ppermute | solution.py:32
  115.6 2.2 constant_dynamic-update-slice_fusion.14
  118.7 1.7 collective-permute-done.15
  120.4 38.9 %collective-permute-start.2 = (bf16[1152,384]{1,0:T(8,128)(2,1)S(1)}, bf16[1152,384]{1,0:T(8,128)(2,1)S(1)}, u32[]{:S(2)}, u32[]{:S(2)}) collective-permute-start(bf16[1152,384]{1,0:T(8,128)(2,1)S(1)} %bitcast.53), channel_id=1, source_target_pairs={{0,8},{4,12},{1,9},{5,13},{2,10},{6,14},{3,11},{7,15},{16,24},{20,... | collective-permute-start | bytes 2654216 | tf_op jit(solution)/shard_map/ppermute | solution.py:32
  160.3 14.4 %collective-permute-done.16 = bf16[1152,384]{1,0:T(8,128)(2,1)S(1)} collective-permute-done((bf16[1152,384]{1,0:T(8,128)(2,1)S(1)}, bf16[1152,384]{1,0:T(8,128)(2,1)S(1)}, u32[]{:S(2)}, u32[]{:S(2)}) %collective-permute-start.16) | collective-permute-done | bytes 884768 | tf_op jit(solution)/shard_map/ppermute | solution.py:32
  174.7 1.3 collective-permute-start.3
  177.1 1.3 collective-permute-start.4
  179.4 1.3 collective-permute-start.5
  181.5 1.3 collective-permute-start.6
  185.5 7.9 %collective-permute-done.3 = bf16[1152,384]{1,0:T(8,128)(2,1)S(1)} collective-permute-done((bf16[1152,384]{1,0:T(8,128)(2,1)S(1)}, bf16[1152,384]{1,0:T(8,128)(2,1)S(1)}, u32[]{:S(2)}, u32[]{:S(2)}) %collective-permute-start.3) | collective-permute-done | bytes 884768 | tf_op jit(solution)/shard_map/ppermute | solution.py:32
  195.4 4.3 %collective-permute-done.4 = bf16[1152,384]{1,0:T(8,128)(2,1)S(1)} collective-permute-done((bf16[1152,384]{1,0:T(8,128)(2,1)S(1)}, bf16[1152,384]{1,0:T(8,128)(2,1)S(1)}, u32[]{:S(2)}, u32[]{:S(2)}) %collective-permute-start.4) | collective-permute-done | bytes 884768 | tf_op jit(solution)/shard_map/ppermute | solution.py:32
  200.7 54.6 %collective-permute-done.5 = bf16[1152,384]{1,0:T(8,128)(2,1)S(1)} collective-permute-done((bf16[1152,384]{1,0:T(8,128)(2,1)S(1)}, bf16[1152,384]{1,0:T(8,128)(2,1)S(1)}, u32[]{:S(2)}, u32[]{:S(2)}) %collective-permute-start.5) | collective-permute-done | bytes 884768 | tf_op jit(solution)/shard_map/ppermute | solution.py:32
  255.3 1.1 constant_dynamic-update-slice_fusion.2
  258.1 76.2 %while.27 = (s32[]{:T(128)}, bf16[3,384,384]{2,1,0:T(8,128)(2,1)}, s32[3]{0:T(128)S(1)}, bf16[3,384,384]{2,1,0:T(8,128)(2,1)}, s32[3,8]{1,0:T(4,128)S(1)}, /*ind...) while((s32[]{:T(128)}, bf16[3,384,384]{2,1,0:T(8,128)(2,1)}, ...), condition=%wide.region_5.6_spmd.clone, body=%wide.region_0.5_spmd.clone.sunk | while | flops 612344704 | bytes 26889600 | solution.py:102
  261.3 4.0 %gather_fusion.1 = bf16[8,384,384]{2,1,0:T(8,128)(2,1)S(1)} fusion(bf16[23,384,384]{2,1,0:T(8,128)(2,1)} %get-tuple-element.426, s32[1024]{0:T(1024)S(1)} %pad_clamp_fusion.2), kind=kCustom, calls=%fused_computation.1.clone.clone.1 | custom fusion | bytes 4718624 | tf_op jit(solution)/shard_map/while/body/eval_jaxpr/gather | solution.py:78
  265.3 5.2 %gather_fusion.2 = bf16[8,384,384]{2,1,0:T(8,128)(2,1)} fusion(bf16[23,384,384]{2,1,0:T(8,128)(2,1)} %get-tuple-element.427, s32[1024]{0:T(1024)S(1)} %pad_clamp_fusion.2), kind=kCustom, calls=%fused_computation.2.clone.clone.1 | custom fusion | bytes 4718624 | tf_op jit(solution)/shard_map/while/body/eval_jaxpr/gather | solution.py:79
  271.5 11.2 %while.28 = (s32[]{:T(128)}, bf16[384,384]{1,0:T(8,128)(2,1)S(1)}, pred[8,384]{1,0:T(8,128)(4,1)}, bf16[384,384]{1,0:T(8,128)(2,1)S(1)}, bf16[3072,384]{1,0:T(8,...) while((s32[]{:T(128)}, bf16[384,384]{1,0:T(8,128)(2,1)S(1)}, ...), condition=%wide.wide.region_4.4_spmd, body=%wide.wide.region_1.3_spmd.sunk | while | flops 612334848 | bytes 15939227 | solution.py:100
  273.2 2.0 fusion.43
  277.0 2.0 fusion.43
  280.7 2.0 fusion.43
  286.7 4.0 %gather_fusion.1 = bf16[8,384,384]{2,1,0:T(8,128)(2,1)S(1)} fusion(bf16[23,384,384]{2,1,0:T(8,128)(2,1)} %get-tuple-element.426, s32[1024]{0:T(1024)S(1)} %pad_clamp_fusion.2), kind=kCustom, calls=%fused_computation.1.clone.clone.1 | custom fusion | bytes 4718624 | tf_op jit(solution)/shard_map/while/body/eval_jaxpr/gather | solution.py:78
  290.7 5.2 %gather_fusion.2 = bf16[8,384,384]{2,1,0:T(8,128)(2,1)} fusion(bf16[23,384,384]{2,1,0:T(8,128)(2,1)} %get-tuple-element.427, s32[1024]{0:T(1024)S(1)} %pad_clamp_fusion.2), kind=kCustom, calls=%fused_computation.2.clone.clone.1 | custom fusion | bytes 4718624 | tf_op jit(solution)/shard_map/while/body/eval_jaxpr/gather | solution.py:79
  296.9 11.2 %while.28 = (s32[]{:T(128)}, bf16[384,384]{1,0:T(8,128)(2,1)S(1)}, pred[8,384]{1,0:T(8,128)(4,1)}, bf16[384,384]{1,0:T(8,128)(2,1)S(1)}, bf16[3072,384]{1,0:T(8,...) while((s32[]{:T(128)}, bf16[384,384]{1,0:T(8,128)(2,1)S(1)}, ...), condition=%wide.wide.region_4.4_spmd, body=%wide.wide.region_1.3_spmd.sunk | while | flops 612334848 | bytes 15939227 | solution.py:100
  298.6 2.0 fusion.43
  302.3 2.0 fusion.43
  306.1 2.0 fusion.43
  312.0 4.0 %gather_fusion.1 = bf16[8,384,384]{2,1,0:T(8,128)(2,1)S(1)} fusion(bf16[23,384,384]{2,1,0:T(8,128)(2,1)} %get-tuple-element.426, s32[1024]{0:T(1024)S(1)} %pad_clamp_fusion.2), kind=kCustom, calls=%fused_computation.1.clone.clone.1 | custom fusion | bytes 4718624 | tf_op jit(solution)/shard_map/while/body/eval_jaxpr/gather | solution.py:78
  316.0 5.2 %gather_fusion.2 = bf16[8,384,384]{2,1,0:T(8,128)(2,1)} fusion(bf16[23,384,384]{2,1,0:T(8,128)(2,1)} %get-tuple-element.427, s32[1024]{0:T(1024)S(1)} %pad_clamp_fusion.2), kind=kCustom, calls=%fused_computation.2.clone.clone.1 | custom fusion | bytes 4718624 | tf_op jit(solution)/shard_map/while/body/eval_jaxpr/gather | solution.py:79
  322.3 11.2 %while.28 = (s32[]{:T(128)}, bf16[384,384]{1,0:T(8,128)(2,1)S(1)}, pred[8,384]{1,0:T(8,128)(4,1)}, bf16[384,384]{1,0:T(8,128)(2,1)S(1)}, bf16[3072,384]{1,0:T(8,...) while((s32[]{:T(128)}, bf16[384,384]{1,0:T(8,128)(2,1)S(1)}, ...), condition=%wide.wide.region_4.4_spmd, body=%wide.wide.region_1.3_spmd.sunk | while | flops 612334848 | bytes 15939227 | solution.py:100
  324.0 2.0 fusion.43
  327.7 2.0 fusion.43
  331.5 2.0 fusion.43
  334.3 16.1 %all_to_all.54 = bf16[4,288,384]{2,1,0:T(8,128)(2,1)S(1)} all-to-all(bf16[4,288,384]{2,1,0:T(8,128)(2,1)} %bitcast.62), channel_id=1, replica_groups=mesh['clips'=2,'ctx'=4,'head'=4] {'head'}, dimensions={0} | all-to-all | bytes 1769472 | tf_op jit(solution)/shard_map/all_to_all | solution.py:104
  (116 shorter events, 44.6 us)
Async XLA Ops:
  0.0 32.9 %copy-start.3 = (s32[3]{0:T(128)S(1)}, s32[3]{0:T(128)}, u32[]{:S(2)}) copy-start(s32[3]{0:T(128)} %param.13) | copy-start | bytes 40
  0.0 18.6 %copy-start = (bf16[288,1536]{1,0:T(8,128)(2,1)S(1)}, bf16[288,1536]{1,0:T(8,128)(2,1)}, u32[]{:S(2)}) copy-start(bf16[288,1536]{1,0:T(8,128)(2,1)} %param.9) | copy-start | bytes 2654212
  0.0 95.0 %copy-start.4 = (s32[3,8]{1,0:T(4,128)S(1)}, s32[3,8]{1,0:T(4,128)}, u32[]{:S(2)}) copy-start(s32[3,8]{1,0:T(4,128)} %param.12) | copy-start | bytes 292
  1.5 18.1 %collective-permute-start.8 = (bf16[288,384]{1,0:T(8,128)(2,1)S(1)}, bf16[288,384]{1,0:T(8,128)(2,1)}, u32[]{:S(2)}, u32[]{:S(2)}) collective-permute-start(bf16[288,384]{1,0:T(8,128)(2,1)S(1)} %get-tuple-element.210), channel_id=1, source_target_pairs={{0,1},{1,0},{2,3},{3,2},{4,5},{5,4},{6,7},{7,6},{8,9},{9,8},{10,11... | collective-permute-start | bytes 663560 | tf_op jit(solution)/shard_map/ppermute | solution.py:24
  2.1 18.5 %collective-permute-start.9 = (bf16[288,384]{1,0:T(8,128)(2,1)S(1)}, bf16[288,384]{1,0:T(8,128)(2,1)}, u32[]{:S(2)}, u32[]{:S(2)}) collective-permute-start(bf16[288,384]{1,0:T(8,128)(2,1)S(1)} %get-tuple-element.212), channel_id=1, source_target_pairs={{0,2},{1,3},{2,0},{3,1},{4,6},{5,7},{6,4},{7,5},{8,10},{9,11},{10,... | collective-permute-start | bytes 663560 | tf_op jit(solution)/shard_map/ppermute | solution.py:24
  4.7 16.9 %collective-permute-start.10 = (bf16[288,384]{1,0:T(8,128)(2,1)S(1)}, bf16[288,384]{1,0:T(8,128)(2,1)S(1)}, u32[]{:S(2)}, u32[]{:S(2)}) collective-permute-start(bf16[288,384]{1,0:T(8,128)(2,1)S(1)} %get-tuple-element.209), channel_id=1, source_target_pairs={{0,3},{1,2},{2,1},{3,0},{4,7},{5,6},{6,5},{7,4},{8,11},{9,10},{10,... | collective-permute-start | bytes 663560 | tf_op jit(solution)/shard_map/ppermute | solution.py:24
  6.9 19.7 %all-to-all-start.1 = ((bf16[288,4,384]{2,0,1:T(8,128)(2,1)}), bf16[288,4,384]{2,0,1:T(8,128)(2,1)S(1)}, u32[]{:S(2)}, u32[]{:S(2)}) async-start(bf16[288,4,384]{2,0,1:T(8,128)(2,1)} %bitcast.33), calls=%async_computation.1 | async-start | bytes 1769472 | tf_op jit(solution)/shard_map/all_to_all | solution.py:44
  10.4 25.5 %collective-permute-start.20 = (s32[3]{0:T(128)}, s32[3]{0:T(128)S(1)}, u32[]{:S(2)}, u32[]{:S(2)}) collective-permute-start(s32[3]{0:T(128)} %param.13), channel_id=1, source_target_pairs={{0,12},{1,13},{2,14},{3,15},{16,28},{17,29},{18,30},{19,31}} | collective-permute-start | bytes 44 | tf_op jit(solution)/shard_map/ppermute | solution.py:32
  17.5 14.3 %collective-permute-start.19 = (s32[1]{0:T(128)}, s32[1]{0:T(128)}, u32[]{:S(2)}, u32[]{:S(2)}) collective-permute-start(s32[1]{0:T(128)} %get-tuple-element.216), channel_id=1, source_target_pairs={} | collective-permute-start | bytes 20 | tf_op jit(solution)/shard_map/ppermute | solution.py:32
  21.7 81.3 %collective-permute-start.12 = (bf16[1152,384]{1,0:T(8,128)(2,1)S(1)}, bf16[1152,384]{1,0:T(8,128)(2,1)S(1)}, u32[]{:S(2)}, u32[]{:S(2)}) collective-permute-start(bf16[1152,384]{1,0:T(8,128)(2,1)S(1)} %constant_dynamic-update-slice_fusion.18), channel_id=1, source_target_pairs={{0,12},{1,13},{2,14},{3,15},{16,28},{17,29},{18,30},{19,31}} | collective-permute-start | bytes 2654216 | tf_op jit(solution)/shard_map/ppermute | solution.py:32
  23.1 82.3 %collective-permute-start.13 = (bf16[1152,384]{1,0:T(8,128)(2,1)S(1)}, bf16[1152,384]{1,0:T(8,128)(2,1)S(1)}, u32[]{:S(2)}, u32[]{:S(2)}) collective-permute-start(bf16[1152,384]{1,0:T(8,128)(2,1)S(1)} %constant_dynamic-update-slice_fusion.18), channel_id=1, source_target_pairs={{0,8},{4,12},{1,9},{5,13},{2,10},{6,14},{3,11},{7,15},{16,24},{20,... | collective-permute-start | bytes 2654216 | tf_op jit(solution)/shard_map/ppermute | solution.py:32
  25.3 71.7 %collective-permute-start.11 = (bf16[384,384]{1,0:T(8,128)(2,1)}, bf16[384,384]{1,0:T(8,128)(2,1)}, u32[]{:S(2)}, u32[]{:S(2)}) collective-permute-start(bf16[384,384]{1,0:T(8,128)(2,1)} %get-tuple-element.208), channel_id=1, source_target_pairs={} | collective-permute-start | bytes 884744 | tf_op jit(solution)/shard_map/ppermute | solution.py:32
  26.6 231.5 %all-to-all-start = ((bf16[288,4,384]{2,0,1:T(8,128)(2,1)}), bf16[288,4,384]{2,0,1:T(8,128)(2,1)}, u32[]{:S(2)}, u32[]{:S(2)}) async-start(bf16[288,4,384]{2,0,1:T(8,128)(2,1)} %bitcast.34), calls=%async_computation | async-start | bytes 1769472 | tf_op jit(solution)/shard_map/all_to_all | solution.py:43
  31.8 1.1 collective-permute-start.26
  32.9 28.7 %collective-permute-start.21 = (s32[3]{0:T(128)S(1)}, s32[3]{0:T(128)S(1)}, u32[]{:S(2)}, u32[]{:S(2)}) collective-permute-start(s32[3]{0:T(128)S(1)} %copy-done.3), channel_id=1, source_target_pairs={{0,8},{4,12},{1,9},{5,13},{2,10},{6,14},{3,11},{7,15},{16,24},{20,... | collective-permute-start | bytes 44 | tf_op jit(solution)/shard_map/ppermute | solution.py:32
  36.0 26.9 %collective-permute-start.22 = (s32[3]{0:T(128)S(1)}, s32[3]{0:T(128)S(1)}, u32[]{:S(2)}, u32[]{:S(2)}) collective-permute-start(s32[3]{0:T(128)S(1)} %copy-done.3), channel_id=1, source_target_pairs={{0,4},{4,8},{8,12},{1,5},{5,9},{9,13},{2,6},{6,10},{10,14},{3,7},{... | collective-permute-start | bytes 44 | tf_op jit(solution)/shard_map/ppermute | solution.py:32
  61.6 31.6 %copy-start.5 = (s32[3]{0:T(128)}, s32[3]{0:T(128)S(1)}, u32[]{:S(2)}) copy-start(s32[3]{0:T(128)S(1)} %collective-permute-done.21) | copy-start | bytes 40
  61.6 23.9 %collective-permute-start.23 = (s32[3]{0:T(128)S(1)}, s32[3]{0:T(128)S(1)}, u32[]{:S(2)}, u32[]{:S(2)}) collective-permute-start(s32[3]{0:T(128)S(1)} %copy-done.3), channel_id=1, source_target_pairs={{4,0},{8,4},{12,8},{5,1},{9,5},{13,9},{6,2},{10,6},{14,10},{7,3},{... | collective-permute-start | bytes 44 | tf_op jit(solution)/shard_map/ppermute | solution.py:32
  62.9 30.3 %copy-start.6 = (s32[3]{0:T(128)}, s32[3]{0:T(128)S(1)}, u32[]{:S(2)}) copy-start(s32[3]{0:T(128)S(1)} %collective-permute-done.22) | copy-start | bytes 40
  62.9 25.3 %collective-permute-start.24 = (s32[3]{0:T(128)S(1)}, s32[3]{0:T(128)S(1)}, u32[]{:S(2)}, u32[]{:S(2)}) collective-permute-start(s32[3]{0:T(128)S(1)} %copy-done.3), channel_id=1, source_target_pairs={{8,0},{12,4},{9,1},{13,5},{10,2},{14,6},{11,3},{15,7},{24,16},{28,... | collective-permute-start | bytes 44 | tf_op jit(solution)/shard_map/ppermute | solution.py:32
  85.4 7.7 %copy-start.7 = (s32[3]{0:T(128)}, s32[3]{0:T(128)S(1)}, u32[]{:S(2)}) copy-start(s32[3]{0:T(128)S(1)} %collective-permute-done.23) | copy-start | bytes 40
  85.4 7.7 %collective-permute-start.25 = (s32[3]{0:T(128)S(1)}, s32[3]{0:T(128)S(1)}, u32[]{:S(2)}, u32[]{:S(2)}) collective-permute-start(s32[3]{0:T(128)S(1)} %copy-done.3), channel_id=1, source_target_pairs={{12,0},{13,1},{14,2},{15,3},{28,16},{29,17},{30,18},{31,19}} | collective-permute-start | bytes 44 | tf_op jit(solution)/shard_map/ppermute | solution.py:32
  88.2 5.0 %copy-start.8 = (s32[3]{0:T(128)}, s32[3]{0:T(128)S(1)}, u32[]{:S(2)}) copy-start(s32[3]{0:T(128)S(1)} %collective-permute-done.24) | copy-start | bytes 40
  88.2 21.9 %collective-permute-start.14 = (bf16[1152,384]{1,0:T(8,128)(2,1)S(1)}, bf16[1152,384]{1,0:T(8,128)(2,1)}, u32[]{:S(2)}, u32[]{:S(2)}) collective-permute-start(bf16[1152,384]{1,0:T(8,128)(2,1)S(1)} %constant_dynamic-update-slice_fusion.18), channel_id=1, source_target_pairs={{0,4},{4,8},{8,12},{1,5},{5,9},{9,13},{2,6},{6,10},{10,14},{3,7},{... | collective-permute-start | bytes 2654216 | tf_op jit(solution)/shard_map/ppermute | solution.py:32
  93.1 0.5 copy-start.9
  93.7 6.3 %collective-permute-start = (bf16[384,384]{1,0:T(8,128)(2,1)}, bf16[384,384]{1,0:T(8,128)(2,1)}, u32[]{:S(2)}, u32[]{:S(2)}) collective-permute-start(bf16[384,384]{1,0:T(8,128)(2,1)} %get-tuple-element.214), channel_id=1, source_target_pairs={} | collective-permute-start | bytes 884744 | tf_op jit(solution)/shard_map/ppermute | solution.py:32
  97.0 23.4 %collective-permute-start.15 = (bf16[1152,384]{1,0:T(8,128)(2,1)S(1)}, bf16[1152,384]{1,0:T(8,128)(2,1)S(1)}, u32[]{:S(2)}, u32[]{:S(2)}) collective-permute-start(bf16[1152,384]{1,0:T(8,128)(2,1)S(1)} %constant_dynamic-update-slice_fusion.18), channel_id=1, source_target_pairs={{4,0},{8,4},{12,8},{5,1},{9,5},{13,9},{6,2},{10,6},{14,10},{7,3},{... | collective-permute-start | bytes 2654216 | tf_op jit(solution)/shard_map/ppermute | solution.py:32
  100.0 74.7 %collective-permute-start.16 = (bf16[1152,384]{1,0:T(8,128)(2,1)S(1)}, bf16[1152,384]{1,0:T(8,128)(2,1)S(1)}, u32[]{:S(2)}, u32[]{:S(2)}) collective-permute-start(bf16[1152,384]{1,0:T(8,128)(2,1)S(1)} %constant_dynamic-update-slice_fusion.18), channel_id=1, source_target_pairs={{8,0},{12,4},{9,1},{13,5},{10,2},{14,6},{11,3},{15,7},{24,16},{28,... | collective-permute-start | bytes 2654216 | tf_op jit(solution)/shard_map/ppermute | solution.py:32
  103.0 74.1 %collective-permute-start.17 = (bf16[1152,384]{1,0:T(8,128)(2,1)S(1)}, bf16[1152,384]{1,0:T(8,128)(2,1)S(1)}, u32[]{:S(2)}, u32[]{:S(2)}) collective-permute-start(bf16[1152,384]{1,0:T(8,128)(2,1)S(1)} %constant_dynamic-update-slice_fusion.18), channel_id=1, source_target_pairs={{12,0},{13,1},{14,2},{15,3},{28,16},{29,17},{30,18},{31,19}} | collective-permute-start | bytes 2654216 | tf_op jit(solution)/shard_map/ppermute | solution.py:32
  105.3 78.4 %copy-start.2 = (bf16[384,384]{1,0:T(8,128)(2,1)S(1)}, bf16[384,384]{1,0:T(8,128)(2,1)}, u32[]{:S(2)}) copy-start(bf16[384,384]{1,0:T(8,128)(2,1)} %get-tuple-element.213) | copy-start | bytes 884740
  105.4 74.1 %collective-permute-start.18 = (bf16[384,384]{1,0:T(8,128)(2,1)}, bf16[384,384]{1,0:T(8,128)(2,1)S(1)}, u32[]{:S(2)}, u32[]{:S(2)}) collective-permute-start(bf16[384,384]{1,0:T(8,128)(2,1)} %get-tuple-element.207), channel_id=1, source_target_pairs={} | collective-permute-start | bytes 884744 | tf_op jit(solution)/shard_map/ppermute | solution.py:32
  110.1 71.3 %collective-permute-start.1 = (bf16[1152,384]{1,0:T(8,128)(2,1)S(1)}, bf16[1152,384]{1,0:T(8,128)(2,1)S(1)}, u32[]{:S(2)}, u32[]{:S(2)}) collective-permute-start(bf16[1152,384]{1,0:T(8,128)(2,1)S(1)} %bitcast.52), channel_id=1, source_target_pairs={{0,12},{1,13},{2,14},{3,15},{16,28},{17,29},{18,30},{19,31}} | collective-permute-start | bytes 2654216 | tf_op jit(solution)/shard_map/ppermute | solution.py:32
  120.4 63.4 %collective-permute-start.2 = (bf16[1152,384]{1,0:T(8,128)(2,1)S(1)}, bf16[1152,384]{1,0:T(8,128)(2,1)S(1)}, u32[]{:S(2)}, u32[]{:S(2)}) collective-permute-start(bf16[1152,384]{1,0:T(8,128)(2,1)S(1)} %bitcast.53), channel_id=1, source_target_pairs={{0,8},{4,12},{1,9},{5,13},{2,10},{6,14},{3,11},{7,15},{16,24},{20,... | collective-permute-start | bytes 2654216 | tf_op jit(solution)/shard_map/ppermute | solution.py:32
  174.7 18.6 %collective-permute-start.3 = (bf16[1152,384]{1,0:T(8,128)(2,1)S(1)}, bf16[1152,384]{1,0:T(8,128)(2,1)S(1)}, u32[]{:S(2)}, u32[]{:S(2)}) collective-permute-start(bf16[1152,384]{1,0:T(8,128)(2,1)S(1)} %bitcast.54), channel_id=1, source_target_pairs={{0,4},{4,8},{8,12},{1,5},{5,9},{9,13},{2,6},{6,10},{10,14},{3,7},{... | collective-permute-start | bytes 2654216 | tf_op jit(solution)/shard_map/ppermute | solution.py:32
  177.1 22.6 %collective-permute-start.4 = (bf16[1152,384]{1,0:T(8,128)(2,1)S(1)}, bf16[1152,384]{1,0:T(8,128)(2,1)S(1)}, u32[]{:S(2)}, u32[]{:S(2)}) collective-permute-start(bf16[1152,384]{1,0:T(8,128)(2,1)S(1)} %bitcast.55), channel_id=1, source_target_pairs={{4,0},{8,4},{12,8},{5,1},{9,5},{13,9},{6,2},{10,6},{14,10},{7,3},{... | collective-permute-start | bytes 2654216 | tf_op jit(solution)/shard_map/ppermute | solution.py:32
  179.4 75.8 %collective-permute-start.5 = (bf16[1152,384]{1,0:T(8,128)(2,1)S(1)}, bf16[1152,384]{1,0:T(8,128)(2,1)S(1)}, u32[]{:S(2)}, u32[]{:S(2)}) collective-permute-start(bf16[1152,384]{1,0:T(8,128)(2,1)S(1)} %bitcast.56), channel_id=1, source_target_pairs={{8,0},{12,4},{9,1},{13,5},{10,2},{14,6},{11,3},{15,7},{24,16},{28,... | collective-permute-start | bytes 2654216 | tf_op jit(solution)/shard_map/ppermute | solution.py:32
  181.5 74.8 %collective-permute-start.6 = (bf16[1152,384]{1,0:T(8,128)(2,1)S(1)}, bf16[1152,384]{1,0:T(8,128)(2,1)S(1)}, u32[]{:S(2)}, u32[]{:S(2)}) collective-permute-start(bf16[1152,384]{1,0:T(8,128)(2,1)S(1)} %bitcast.57), channel_id=1, source_target_pairs={{12,0},{13,1},{14,2},{15,3},{28,16},{29,17},{30,18},{31,19}} | collective-permute-start | bytes 2654216 | tf_op jit(solution)/shard_map/ppermute | solution.py:32
  183.8 73.5 %collective-permute-start.7 = (bf16[384,384]{1,0:T(8,128)(2,1)S(1)}, bf16[384,384]{1,0:T(8,128)(2,1)S(1)}, u32[]{:S(2)}, u32[]{:S(2)}) collective-permute-start(bf16[384,384]{1,0:T(8,128)(2,1)S(1)} %copy-done.2), channel_id=1, source_target_pairs={} | collective-permute-start | bytes 884744 | tf_op jit(solution)/shard_map/ppermute | solution.py:32
  261.2 10.2 %copy-start.1 = (pred[8,384]{1,0:T(8,128)(4,1)}, pred[8,384]{1,0:T(8,128)(4,1)S(1)}, u32[]{:S(2)}) copy-start(pred[8,384]{1,0:T(8,128)(4,1)S(1)} %gather_fusion) | copy-start | bytes 9220 | tf_op jit(solution)/shard_map/while
  286.6 10.2 %copy-start.1 = (pred[8,384]{1,0:T(8,128)(4,1)}, pred[8,384]{1,0:T(8,128)(4,1)S(1)}, u32[]{:S(2)}) copy-start(pred[8,384]{1,0:T(8,128)(4,1)S(1)} %gather_fusion) | copy-start | bytes 9220 | tf_op jit(solution)/shard_map/while
  312.0 10.2 %copy-start.1 = (pred[8,384]{1,0:T(8,128)(4,1)}, pred[8,384]{1,0:T(8,128)(4,1)S(1)}, u32[]{:S(2)}) copy-start(pred[8,384]{1,0:T(8,128)(4,1)S(1)} %gather_fusion) | copy-start | bytes 9220 | tf_op jit(solution)/shard_map/while
